TPU v7x, 256 devices: a whole 4x4x8 slice. The times are simulated.
256 devices in a mesh: tile: 32 (over x_lo, z, core), mlp: 8 (over y, x_hi).
Axes of the slice: x: 4 (x_hi: 2, x_lo: 2; x = x_hi * 2 + x_lo), y: 4, z: 8, core: 2. Of those that a mesh axis runs over, the one named last changes fastest.
Arguments:
- features: bfloat16 [32, 512, 2, 2, 256], P('tile', 'mlp'), may hold values from -6 to 6
- w_in: bfloat16 [256, 1024], P(None, 'mlp'), may hold values from -0.375 to 0.375
- w_out: bfloat16 [1024, 256], P('mlp'), may hold values from -0.1875 to 0.1875
- bilinear: bfloat16 [256, 256], replicated, may hold values from -0.375 to 0.375
- partner: int32 [32, 2, 512], replicated, may hold values from 0 to 13823
- counts: int32 [32, 2, 2], replicated, may hold values from 128 to 512
Outputs:
- pair_loss: float32 [], replicated
- grad_in: float32 [256, 1024], P(None, 'mlp')
- grad_out: float32 [1024, 256], P('mlp')
- grad_bilinear: float32 [256, 256], replicated
All inputs are finite; a program needn't handle non-finite values.
Results may differ from a plain program's by a relative error of at most 0.0024.
The roundings to bfloat16 on the way count: a program that leaves them out, or rounds other values in their place, can miss the bound.
Values may be sent and summed in bfloat16 or wider, within the bound.
A program may use at most 64 MiB of HBM per device.

v0:
```python
import jax
import jax.numpy as jnp
from jax import lax
from jax.sharding import PartitionSpec as P

column_plan = ((-1, 1), (0, 0), (0, 1), (1, 0))


def shifted(array, axis, by):
    peers = lax.axis_size(axis)
    pairs = [(i, i + by) for i in range(peers) if 0 <= i + by < peers]
    return lax.ppermute(array, axis, pairs)


def pair_slope(raw_score, target, weight, heavy_weight, factor):
    chance = jax.nn.sigmoid(raw_score)
    signed = (1.0 - target) * chance - heavy_weight * target * (1.0 - chance)
    return (weight * signed * factor).astype(jnp.bfloat16)


def pair_cost(raw_score, target, weight, heavy_weight):
    missed = heavy_weight * target * jnp.log1p(jnp.exp(-raw_score))
    spurious = (1.0 - target) * jnp.log1p(jnp.exp(raw_score))
    return jnp.sum(weight * (missed + spurious))


def local(features, w_in, w_out, bilinear, partner, counts):
    row_part = features.shape[1]
    feature_width = features.shape[4]
    groups = lax.axis_size("mlp")
    site_rows = row_part * groups
    tile_count = lax.axis_size("tile")
    grid_depth = tile_count // 8
    tile_here = lax.axis_index("tile")
    member = lax.axis_index("mlp")
    block_x = tile_here // (4 * grid_depth)
    block_y = tile_here // grid_depth % 4
    block_z = tile_here % grid_depth
    heavy_weight = 27 * site_rows // 4
    score_scale = feature_width ** (-0.5)
    factor = score_scale / (2 * tile_count * site_rows)
    own_rows = member * row_part + jnp.arange(row_part, dtype=jnp.int32)
    all_rows = jnp.arange(site_rows, dtype=jnp.int32)
    mine_counts = lax.dynamic_index_in_dim(counts, tile_here, 0, keepdims=False)
    mine_partner = lax.dynamic_index_in_dim(partner, tile_here, 0, keepdims=False)
    own_partner = lax.dynamic_slice_in_dim(mine_partner, member * row_part, row_part, 1)
    own_pre_ok = own_rows[None, :] < mine_counts[:, 0:1]
    own_post_ok = own_rows[None, :] < mine_counts[:, 1:2]
    local_x = features.reshape(row_part, 4, feature_width)
    whole_x = lax.all_gather(local_x, "mlp", axis=0, tiled=True)
    hidden_pre = jnp.einsum("rcf,fh->rch", whole_x, w_in, preferred_element_type=jnp.float32)
    active = jax.nn.gelu(hidden_pre).astype(jnp.bfloat16)
    mixed_rows = lax.psum_scatter(
        jnp.einsum("rch,hf->rcf", active, w_out, preferred_element_type=jnp.float32),
        "mlp",
        scatter_dimension=0,
        tiled=True,
    )
    embedded = (local_x.astype(jnp.float32) + mixed_rows).astype(jnp.bfloat16)
    pre_local = embedded[:, 0::2]
    post_local = embedded[:, 1::2]
    query_local = jnp.einsum(
        "ruf,fg->rug", pre_local, bilinear, preferred_element_type=jnp.float32
    ).astype(jnp.bfloat16)

    def pair_code(step_x, step_y, step_z):
        return ((step_x + 1) * 9 + (step_y + 1) * 3 + step_z + 1) * site_rows

    loss_sum = jnp.zeros((), jnp.float32)
    post_grads = [
        jnp.zeros((row_part, feature_width), jnp.float32),
        jnp.zeros((row_part, feature_width), jnp.float32),
    ]
    post_whole, query_whole = (
        lax.all_gather(post_local, "mlp", axis=0, tiled=True),
        lax.all_gather(query_local, "mlp", axis=0, tiled=True),
    )
    query_grads = [
        jnp.zeros((row_part, feature_width), jnp.float32),
        jnp.zeros((row_part, feature_width), jnp.float32),
    ]
    for step_y in (-1, 0, 1):
        for step_z in (-1, 0, 1):
            post_cols, query_cols, post_valid, pre_valid, label_cols = ([], [], [], [], [])
            for position in range(4):
                shift_x, sub_tile = column_plan[position]
                offset = shift_x * 4 * grid_depth + step_y * grid_depth + step_z
                inside = (
                    (block_x + shift_x >= 0)
                    & (block_x + shift_x < 2)
                    & (block_y + step_y >= 0)
                    & (block_y + step_y < 4)
                    & (block_z + step_z >= 0)
                    & (block_z + step_z < grid_depth)
                )
                source = jnp.clip(tile_here + offset, 0, tile_count - 1)
                tile_counts = lax.dynamic_index_in_dim(counts, source, 0, keepdims=False)[sub_tile]
                labels = lax.dynamic_index_in_dim(partner, source, 0, keepdims=False)[sub_tile]
                offset, sub_tile, inside, tile_counts, labels = (
                    offset,
                    sub_tile,
                    inside,
                    tile_counts,
                    labels,
                )
                both_sides = jnp.stack([post_whole[:, sub_tile], query_whole[:, sub_tile]], 0)
                if offset != 0:
                    both_sides = shifted(both_sides, "tile", -offset)
                post_cols.append(both_sides[0])
                query_cols.append(both_sides[1])
                post_valid.append(inside & (all_rows < tile_counts[1]))
                pre_valid.append(inside & (all_rows < tile_counts[0]))
                label_cols.append(labels)
            for pretile in (0, 1):
                chosen = range(pretile, pretile + 3)
                others = jnp.concatenate([post_cols[column_id] for column_id in chosen], 0)
                col_key = jnp.concatenate(
                    [
                        pair_code(column_id - 1 - pretile, step_y, step_z) + all_rows
                        for column_id in chosen
                    ]
                )
                col_ok = jnp.concatenate([post_valid[column_id] for column_id in chosen])
                raw_score = (
                    jnp.einsum(
                        "rf,cf->rc",
                        query_local[:, pretile],
                        others,
                        preferred_element_type=jnp.float32,
                    )
                    * score_scale
                )
                target = (own_partner[pretile][:, None] == col_key[None, :]).astype(jnp.float32)
                weight = (own_pre_ok[pretile][:, None] & col_ok[None, :]).astype(jnp.float32)
                loss_sum = loss_sum + pair_cost(raw_score, target, weight, heavy_weight)
                slope = pair_slope(raw_score, target, weight, heavy_weight, factor)
                query_grads[pretile] = query_grads[pretile] + jnp.dot(
                    slope, others, preferred_element_type=jnp.float32
                )
                senders = jnp.concatenate([query_cols[column_id] for column_id in chosen], 0)
                row_key = jnp.concatenate(
                    [
                        label_cols[column_id] - pair_code(pretile - column_id + 1, -step_y, -step_z)
                        for column_id in chosen
                    ]
                )
                row_ok = jnp.concatenate([pre_valid[column_id] for column_id in chosen])
                back_score = (
                    jnp.einsum(
                        "cf,rf->cr",
                        post_local[:, pretile],
                        senders,
                        preferred_element_type=jnp.float32,
                    )
                    * score_scale
                )
                back_target = (own_rows[:, None] == row_key[None, :]).astype(jnp.float32)
                back_weight = (own_post_ok[pretile][:, None] & row_ok[None, :]).astype(jnp.float32)
                back_slope = pair_slope(back_score, back_target, back_weight, heavy_weight, factor)
                post_grads[pretile] = post_grads[pretile] + jnp.dot(
                    back_slope, senders, preferred_element_type=jnp.float32
                )
    query_total = jnp.stack(query_grads, 1)
    query_back = query_total.astype(jnp.bfloat16)
    post_back = jnp.stack(post_grads, 1)
    bilinear_part = jnp.einsum(
        "ruf,rug->fg", pre_local, query_back, preferred_element_type=jnp.float32
    )
    pre_back = jnp.einsum("rug,fg->ruf", query_back, bilinear, preferred_element_type=jnp.float32)
    embed_grad = jnp.stack(
        [pre_back[:, 0], post_back[:, 0], pre_back[:, 1], post_back[:, 1]], 1
    ).astype(jnp.bfloat16)
    embed_whole = lax.all_gather(embed_grad, "mlp", axis=0, tiled=True)
    active_grad = jnp.einsum("rcf,hf->rch", embed_whole, w_out, preferred_element_type=jnp.float32)
    unused, pullback = jax.vjp(jax.nn.gelu, hidden_pre)
    hidden_grad = pullback(active_grad)[0].astype(jnp.bfloat16)
    in_part = jnp.einsum("rcf,rch->fh", whole_x, hidden_grad, preferred_element_type=jnp.float32)
    out_part = jnp.einsum("rch,rcf->hf", active, embed_whole, preferred_element_type=jnp.float32)
    grad_in, grad_out = lax.psum((in_part, out_part), "tile")
    grad_bilinear, loss_total = lax.psum((bilinear_part, loss_sum), ("tile", "mlp"))
    pair_loss = loss_total / (2.0 * tile_count * site_rows * 27 * site_rows)
    return (pair_loss, grad_in, grad_out, grad_bilinear)


def solution(mesh):
    placed = (P("tile", "mlp", None, None, None), P(None, "mlp"), P("mlp", None), P(), P(), P())
    return jax.shard_map(
        local,
        mesh=mesh,
        in_specs=placed,
        out_specs=(P(), P(None, "mlp"), P("mlp", None), P()),
        check_vma=False,
    )
```

profile of v0, /device:TPU:2, one launch (start us, length us, event | category | flops | bytes accessed | tf_op | source)
XLA Modules:
  0.0 1315.0 jit_solution(17551962125909204225)
XLA Ops:
  85.1 70.2 %reduce-scatter.2.cloned.1.call-done = f32[64,4,256]{2,0,1:T(8,128)} async-done(((f32[512,4,256]{2,0,1:T(8,128)}), f32[64,4,256]{2,0,1:T(8,128)}) %reduce-scatter.2.cloned.1.call-update) | async-done | bytes 262160 | tf_op jit(solution)/shard_map/reduce_scatter | solution.py:53
  156.3 35.8 %all_gather.13 = bf16[512,2,256]{2,0,1:T(8,128)(2,1)S(1)} all-gather(bf16[64,2,256]{2,0,1:T(8,128)(2,1)S(1)} %slice.1000), channel_id=1, replica_groups=mesh['tile'=32,'mlp'=8] {'mlp'}, dimensions={0}, use_global_device_ids=true | all-gather | bytes 589824 | tf_op jit(solution)/shard_map/all_gather | solution.py:75
  192.4 35.4 %all_gather.14 = bf16[512,2,256]{2,0,1:T(8,128)(2,1)S(1)} all-gather(bf16[64,2,256]{2,0,1:T(8,128)(2,1)S(1)} %convolution_convert_fusion.1), channel_id=1, replica_groups=mesh['tile'=32,'mlp'=8] {'mlp'}, dimensions={0}, use_global_device_ids=true | all-gather | bytes 589824 | tf_op jit(solution)/shard_map/all_gather | solution.py:76
  255.3 33.1 %collective-permute-done.6 = bf16[2,512,256]{2,1,0:T(8,128)(2,1)S(1)} collective-permute-done((bf16[2,512,256]{2,1,0:T(8,128)(2,1)S(1)}, bf16[2,512,256]{2,1,0:T(8,128)(2,1)S(1)}, u32[]{:S(2)}, u32[]{:S(2)}) %collective-permute-start.6) | collective-permute-done | bytes 524320 | tf_op jit(solution)/shard_map/ppermute | solution.py:12
  294.6 9.4 collective-permute-start.10
  304.8 26.9 %collective-permute-done.2 = bf16[2,512,256]{2,1,0:T(8,128)(2,1)S(1)} collective-permute-done((bf16[2,512,256]{2,1,0:T(8,128)(2,1)S(1)}, bf16[2,512,256]{2,1,0:T(8,128)(2,1)S(1)}, u32[]{:S(2)}, u32[]{:S(2)}) %collective-permute-start.2) | collective-permute-done | bytes 524320 | tf_op jit(solution)/shard_map/ppermute | solution.py:12
  331.8 12.9 collective-permute-start.13
  348.1 14.5 %collective-permute-done.10 = bf16[2,512,256]{2,1,0:T(8,128)(2,1)S(1)} collective-permute-done((bf16[2,512,256]{2,1,0:T(8,128)(2,1)S(1)}, bf16[2,512,256]{2,1,0:T(8,128)(2,1)S(1)}, u32[]{:S(2)}, u32[]{:S(2)}) %collective-permute-start.10) | collective-permute-done | bytes 524320 | tf_op jit(solution)/shard_map/ppermute | solution.py:12
  364.6 37.0 %collective-permute-start.19 = (bf16[2,512,256]{2,1,0:T(8,128)(2,1)S(1)}, bf16[2,512,256]{2,1,0:T(8,128)(2,1)S(1)}, u32[]{:S(2)}, u32[]{:S(2)}) collective-permute-start(bf16[2,512,256]{2,1,0:T(8,128)(2,1)S(1)} %pad_maximum_fusion.37), channel_id=1, source_target_pairs={{8,0},{16,8},{24,16},{32,24},{40,32},{48,40},{56,48},{64,56},{72,6... | collective-permute-start | bytes 1572872 | tf_op jit(solution)/shard_map/ppermute | solution.py:12
  406.5 34.3 %collective-permute-start.18 = (bf16[2,512,256]{2,1,0:T(8,128)(2,1)S(1)}, bf16[2,512,256]{2,1,0:T(8,128)(2,1)S(1)}, u32[]{:S(2)}, u32[]{:S(2)}) collective-permute-start(bf16[2,512,256]{2,1,0:T(8,128)(2,1)S(1)} %pad_maximum_fusion.36), channel_id=1, source_target_pairs={{0,120},{8,128},{16,136},{24,144},{32,152},{40,160},{48,168},{56,1... | collective-permute-start | bytes 1572872 | tf_op jit(solution)/shard_map/ppermute | solution.py:12
  471.6 25.0 %collective-permute-done.24 = bf16[2,512,256]{2,1,0:T(8,128)(2,1)S(1)} collective-permute-done((bf16[2,512,256]{2,1,0:T(8,128)(2,1)S(1)}, bf16[2,512,256]{2,1,0:T(8,128)(2,1)S(1)}, u32[]{:S(2)}, u32[]{:S(2)}) %collective-permute-start.24) | collective-permute-done | bytes 524320 | tf_op jit(solution)/shard_map/ppermute | solution.py:12
  499.3 16.6 %collective-permute-done.22 = bf16[2,512,256]{2,1,0:T(8,128)(2,1)S(1)} collective-permute-done((bf16[2,512,256]{2,1,0:T(8,128)(2,1)S(1)}, bf16[2,512,256]{2,1,0:T(8,128)(2,1)S(1)}, u32[]{:S(2)}, u32[]{:S(2)}) %collective-permute-start.22) | collective-permute-done | bytes 524320 | tf_op jit(solution)/shard_map/ppermute | solution.py:12
  517.4 20.6 %collective-permute-done.27 = bf16[2,512,256]{2,1,0:T(8,128)(2,1)S(1)} collective-permute-done((bf16[2,512,256]{2,1,0:T(8,128)(2,1)S(1)}, bf16[2,512,256]{2,1,0:T(8,128)(2,1)S(1)}, u32[]{:S(2)}, u32[]{:S(2)}) %collective-permute-start.27) | collective-permute-done | bytes 524320 | tf_op jit(solution)/shard_map/ppermute | solution.py:12
  542.8 12.0 collective-permute-done.28
  559.7 14.3 %collective-permute-done.26 = bf16[2,512,256]{2,1,0:T(8,128)(2,1)S(1)} collective-permute-done((bf16[2,512,256]{2,1,0:T(8,128)(2,1)S(1)}, bf16[2,512,256]{2,1,0:T(8,128)(2,1)S(1)}, u32[]{:S(2)}, u32[]{:S(2)}) %collective-permute-start.26) | collective-permute-done | bytes 524320 | tf_op jit(solution)/shard_map/ppermute | solution.py:12
  574.0 27.5 %collective-permute-start.32 = (bf16[2,512,256]{2,1,0:T(8,128)(2,1)S(1)}, bf16[2,512,256]{2,1,0:T(8,128)(2,1)S(1)}, u32[]{:S(2)}, u32[]{:S(2)}) collective-permute-start(bf16[2,512,256]{2,1,0:T(8,128)(2,1)S(1)} %pad_maximum_fusion.36), channel_id=1, source_target_pairs={{40,0},{48,8},{56,16},{64,24},{72,32},{80,40},{88,48},{96,56},{104... | collective-permute-start | bytes 1572872 | tf_op jit(solution)/shard_map/ppermute | solution.py:12
  602.6 28.6 %collective-permute-start.30 = (bf16[2,512,256]{2,1,0:T(8,128)(2,1)S(1)}, bf16[2,512,256]{2,1,0:T(8,128)(2,1)S(1)}, u32[]{:S(2)}, u32[]{:S(2)}) collective-permute-start(bf16[2,512,256]{2,1,0:T(8,128)(2,1)S(1)} %pad_maximum_fusion.36), channel_id=1, source_target_pairs={{0,88},{8,96},{16,104},{24,112},{32,120},{40,128},{48,136},{56,144... | collective-permute-start | bytes 1572872 | tf_op jit(solution)/shard_map/ppermute | solution.py:12
  642.1 16.8 %collective-permute-done.7 = bf16[2,512,256]{2,1,0:T(8,128)(2,1)S(1)} collective-permute-done((bf16[2,512,256]{2,1,0:T(8,128)(2,1)S(1)}, bf16[2,512,256]{2,1,0:T(8,128)(2,1)S(1)}, u32[]{:S(2)}, u32[]{:S(2)}) %collective-permute-start.7) | collective-permute-done | bytes 524320 | tf_op jit(solution)/shard_map/ppermute | solution.py:12
  658.9 13.2 %collective-permute-start.15 = (bf16[2,512,256]{2,1,0:T(8,128)(2,1)S(1)}, bf16[2,512,256]{2,1,0:T(8,128)(2,1)S(1)}, u32[]{:S(2)}, u32[]{:S(2)}) collective-permute-start(bf16[2,512,256]{2,1,0:T(8,128)(2,1)S(1)} %pad_maximum_fusion.37), channel_id=1, source_target_pairs={{120,0},{128,8},{136,16},{144,24},{152,32},{160,40},{168,48},{176,... | collective-permute-start | bytes 1572872 | tf_op jit(solution)/shard_map/ppermute | solution.py:12
  676.7 21.2 %collective-permute-start.17 = (bf16[2,512,256]{2,1,0:T(8,128)(2,1)S(1)}, bf16[2,512,256]{2,1,0:T(8,128)(2,1)S(1)}, u32[]{:S(2)}, u32[]{:S(2)}) collective-permute-start(bf16[2,512,256]{2,1,0:T(8,128)(2,1)S(1)} %pad_maximum_fusion.37), channel_id=1, source_target_pairs={{128,0},{136,8},{144,16},{152,24},{160,32},{168,40},{176,48},{184,... | collective-permute-start | bytes 1572872 | tf_op jit(solution)/shard_map/ppermute | solution.py:12
  753.4 70.2 %all-gather.5.cloned.1.call-done = bf16[512,4,256]{2,0,1:T(8,128)(2,1)} async-done(((bf16[64,4,256]{2,0,1:T(8,128)(2,1)}), bf16[512,4,256]{2,0,1:T(8,128)(2,1)}) %all-gather.5.cloned.1.call-update) | async-done | bytes 1048592 | tf_op jit(solution)/shard_map/all_gather | solution.py:173
  840.1 75.1 %psum.28 = f32[]{:T(128)} all-reduce(f32[]{:T(128)S(6)} %add.976), channel_id=1, replica_groups=mesh['tile'=32,'mlp'=8] {'tile','mlp'}, use_global_device_ids=true, to_apply=%region_19.20 | all-reduce | flops 1 | bytes 8 | tf_op jit(solution)/shard_map/psum | solution.py:180
  915.8 131.6 %all-reduce.6.cloned.1.call-done = (f32[256,128]{0,1:T(8,128)}, f32[128,256]{1,0:T(8,128)}) async-done(((f32[256,128]{0,1:T(8,128)}, f32[128,256]{1,0:T(8,128)}), (f32[256,128]{0,1:T(8,128)}, f32[128,256]{1,0:T(8,128)})) %all-reduce.6.cloned.1.call-update) | async-done | bytes 262160 | tf_op jit(solution)/shard_map/psum | solution.py:179
  1049.0 254.7 %all-reduce.4.cloned.1.call-done = f32[256,256]{1,0:T(8,128)} async-done(((f32[256,256]{1,0:T(8,128)}), f32[256,256]{1,0:T(8,128)}) %all-reduce.4.cloned.1.call-update) | async-done | bytes 262160 | tf_op jit(solution)/shard_map/psum | solution.py:180
  (470 shorter events, 248.2 us)
Async XLA Ops:
  7.2 61.9 %all-gather.3.cloned.1.call-start = ((), (), s32[]{:S(2)}) async-start(), calls=%async_computation.1 | async-start | bytes 1179648 | tf_op jit(solution)/shard_map/all_gather | solution.py:50
  8.9 146.5 %reduce-scatter.2.cloned.1.call-start = ((), (), s32[]{:S(2)}) async-start(), calls=%async_computation.2 | async-start | bytes 2359296 | tf_op jit(solution)/shard_map/reduce_scatter | solution.py:53
  72.6 750.9 %all-gather.5.cloned.1.call-start = ((), (), s32[]{:S(2)}) async-start(), calls=%async_computation.3 | async-start | bytes 1179648 | tf_op jit(solution)/shard_map/all_gather | solution.py:173
  241.5 62.6 %collective-permute-start.1 = (bf16[2,512,256]{2,1,0:T(8,128)(2,1)S(1)}, bf16[2,512,256]{2,1,0:T(8,128)(2,1)S(1)}, u32[]{:S(2)}, u32[]{:S(2)}) collective-permute-start(bf16[2,512,256]{2,1,0:T(8,128)(2,1)S(1)} %pad_maximum_fusion.37), channel_id=1, source_target_pairs={{0,40},{8,48},{16,56},{24,64},{32,72},{40,80},{48,88},{56,96},{64,... | collective-permute-start | bytes 1572872 | tf_op jit(solution)/shard_map/ppermute | solution.py:12
  243.4 88.4 %collective-permute-start.2 = (bf16[2,512,256]{2,1,0:T(8,128)(2,1)S(1)}, bf16[2,512,256]{2,1,0:T(8,128)(2,1)S(1)}, u32[]{:S(2)}, u32[]{:S(2)}) collective-permute-start(bf16[2,512,256]{2,1,0:T(8,128)(2,1)S(1)} %pad_maximum_fusion.36), channel_id=1, source_target_pairs={{0,40},{8,48},{16,56},{24,64},{32,72},{40,80},{48,88},{56,96},{64,... | collective-permute-start | bytes 1572872 | tf_op jit(solution)/shard_map/ppermute | solution.py:12
  254.6 90.1 %collective-permute-start = (bf16[2,512,256]{2,1,0:T(8,128)(2,1)S(1)}, bf16[2,512,256]{2,1,0:T(8,128)(2,1)S(1)}, u32[]{:S(2)}, u32[]{:S(2)}) collective-permute-start(bf16[2,512,256]{2,1,0:T(8,128)(2,1)S(1)} %pad_maximum_fusion.36), channel_id=1, source_target_pairs={{0,168},{8,176},{16,184},{24,192},{32,200},{40,208},{48,216},{56,2... | collective-permute-start | bytes 1572872 | tf_op jit(solution)/shard_map/ppermute | solution.py:12
  288.4 59.0 %collective-permute-start.9 = (bf16[2,512,256]{2,1,0:T(8,128)(2,1)S(1)}, bf16[2,512,256]{2,1,0:T(8,128)(2,1)S(1)}, u32[]{:S(2)}, u32[]{:S(2)}) collective-permute-start(bf16[2,512,256]{2,1,0:T(8,128)(2,1)S(1)} %pad_maximum_fusion.37), channel_id=1, source_target_pairs={{0,24},{8,32},{16,40},{24,48},{32,56},{40,64},{48,72},{56,80},{64,... | collective-permute-start | bytes 1572872 | tf_op jit(solution)/shard_map/ppermute | solution.py:12
  294.6 68.0 %collective-permute-start.10 = (bf16[2,512,256]{2,1,0:T(8,128)(2,1)S(1)}, bf16[2,512,256]{2,1,0:T(8,128)(2,1)S(1)}, u32[]{:S(2)}, u32[]{:S(2)}) collective-permute-start(bf16[2,512,256]{2,1,0:T(8,128)(2,1)S(1)} %pad_maximum_fusion.36), channel_id=1, source_target_pairs={{0,24},{8,32},{16,40},{24,48},{32,56},{40,64},{48,72},{56,80},{64,... | collective-permute-start | bytes 1572872 | tf_op jit(solution)/shard_map/ppermute | solution.py:12
  304.1 60.6 %collective-permute-start.8 = (bf16[2,512,256]{2,1,0:T(8,128)(2,1)S(1)}, bf16[2,512,256]{2,1,0:T(8,128)(2,1)S(1)}, u32[]{:S(2)}, u32[]{:S(2)}) collective-permute-start(bf16[2,512,256]{2,1,0:T(8,128)(2,1)S(1)} %pad_maximum_fusion.36), channel_id=1, source_target_pairs={{0,152},{8,160},{16,168},{24,176},{32,184},{40,192},{48,200},{56,2... | collective-permute-start | bytes 1572872 | tf_op jit(solution)/shard_map/ppermute | solution.py:12
  331.8 70.7 %collective-permute-start.13 = (bf16[2,512,256]{2,1,0:T(8,128)(2,1)S(1)}, bf16[2,512,256]{2,1,0:T(8,128)(2,1)S(1)}, u32[]{:S(2)}, u32[]{:S(2)}) collective-permute-start(bf16[2,512,256]{2,1,0:T(8,128)(2,1)S(1)} %pad_maximum_fusion.37), channel_id=1, source_target_pairs={{0,8},{8,16},{16,24},{24,32},{32,40},{40,48},{48,56},{56,64},{64,7... | collective-permute-start | bytes 1572872 | tf_op jit(solution)/shard_map/ppermute | solution.py:12
  344.7 61.8 %collective-permute-start.14 = (bf16[2,512,256]{2,1,0:T(8,128)(2,1)S(1)}, bf16[2,512,256]{2,1,0:T(8,128)(2,1)S(1)}, u32[]{:S(2)}, u32[]{:S(2)}) collective-permute-start(bf16[2,512,256]{2,1,0:T(8,128)(2,1)S(1)} %pad_maximum_fusion.36), channel_id=1, source_target_pairs={{0,8},{8,16},{16,24},{24,32},{32,40},{40,48},{48,56},{56,64},{64,7... | collective-permute-start | bytes 1572872 | tf_op jit(solution)/shard_map/ppermute | solution.py:12
  347.4 284.9 %collective-permute-start.12 = (bf16[2,512,256]{2,1,0:T(8,128)(2,1)S(1)}, bf16[2,512,256]{2,1,0:T(8,128)(2,1)S(1)}, u32[]{:S(2)}, u32[]{:S(2)}) collective-permute-start(bf16[2,512,256]{2,1,0:T(8,128)(2,1)S(1)} %pad_maximum_fusion.36), channel_id=1, source_target_pairs={{0,136},{8,144},{16,152},{24,160},{32,168},{40,176},{48,184},{56,1... | collective-permute-start | bytes 1572872 | tf_op jit(solution)/shard_map/ppermute | solution.py:12
  362.6 272.7 %collective-permute-start.16 = (bf16[2,512,256]{2,1,0:T(8,128)(2,1)S(1)}, bf16[2,512,256]{2,1,0:T(8,128)(2,1)S(1)}, u32[]{:S(2)}, u32[]{:S(2)}) collective-permute-start(bf16[2,512,256]{2,1,0:T(8,128)(2,1)S(1)} %pad_maximum_fusion.36), channel_id=1, source_target_pairs={{0,128},{8,136},{16,144},{24,152},{32,160},{40,168},{48,176},{56,1... | collective-permute-start | bytes 1572872 | tf_op jit(solution)/shard_map/ppermute | solution.py:12
  364.6 77.0 %collective-permute-start.19 = (bf16[2,512,256]{2,1,0:T(8,128)(2,1)S(1)}, bf16[2,512,256]{2,1,0:T(8,128)(2,1)S(1)}, u32[]{:S(2)}, u32[]{:S(2)}) collective-permute-start(bf16[2,512,256]{2,1,0:T(8,128)(2,1)S(1)} %pad_maximum_fusion.37), channel_id=1, source_target_pairs={{8,0},{16,8},{24,16},{32,24},{40,32},{48,40},{56,48},{64,56},{72,6... | collective-permute-start | bytes 1572872 | tf_op jit(solution)/shard_map/ppermute | solution.py:12
  455.1 60.8 %collective-permute-start.22 = (bf16[2,512,256]{2,1,0:T(8,128)(2,1)S(1)}, bf16[2,512,256]{2,1,0:T(8,128)(2,1)S(1)}, u32[]{:S(2)}, u32[]{:S(2)}) collective-permute-start(bf16[2,512,256]{2,1,0:T(8,128)(2,1)S(1)} %pad_maximum_fusion.36), channel_id=1, source_target_pairs={{0,104},{8,112},{16,120},{24,128},{32,136},{40,144},{48,152},{56,1... | collective-permute-start | bytes 1572872 | tf_op jit(solution)/shard_map/ppermute | solution.py:12
  466.7 71.3 %collective-permute-start.27 = (bf16[2,512,256]{2,1,0:T(8,128)(2,1)S(1)}, bf16[2,512,256]{2,1,0:T(8,128)(2,1)S(1)}, u32[]{:S(2)}, u32[]{:S(2)}) collective-permute-start(bf16[2,512,256]{2,1,0:T(8,128)(2,1)S(1)} %pad_maximum_fusion.37), channel_id=1, source_target_pairs={{32,0},{40,8},{48,16},{56,24},{64,32},{72,40},{80,48},{88,56},{96,... | collective-permute-start | bytes 1572872 | tf_op jit(solution)/shard_map/ppermute | solution.py:12
  496.7 58.2 %collective-permute-start.28 = (bf16[2,512,256]{2,1,0:T(8,128)(2,1)S(1)}, bf16[2,512,256]{2,1,0:T(8,128)(2,1)S(1)}, u32[]{:S(2)}, u32[]{:S(2)}) collective-permute-start(bf16[2,512,256]{2,1,0:T(8,128)(2,1)S(1)} %pad_maximum_fusion.36), channel_id=1, source_target_pairs={{32,0},{40,8},{48,16},{56,24},{64,32},{72,40},{80,48},{88,56},{96,... | collective-permute-start | bytes 1572872 | tf_op jit(solution)/shard_map/ppermute | solution.py:12
  554.9 82.3 %collective-permute-start.31 = (bf16[2,512,256]{2,1,0:T(8,128)(2,1)S(1)}, bf16[2,512,256]{2,1,0:T(8,128)(2,1)S(1)}, u32[]{:S(2)}, u32[]{:S(2)}) collective-permute-start(bf16[2,512,256]{2,1,0:T(8,128)(2,1)S(1)} %pad_maximum_fusion.37), channel_id=1, source_target_pairs={{40,0},{48,8},{56,16},{64,24},{72,32},{80,40},{88,48},{96,56},{104... | collective-permute-start | bytes 1572872 | tf_op jit(solution)/shard_map/ppermute | solution.py:12
  574.0 102.6 %collective-permute-start.32 = (bf16[2,512,256]{2,1,0:T(8,128)(2,1)S(1)}, bf16[2,512,256]{2,1,0:T(8,128)(2,1)S(1)}, u32[]{:S(2)}, u32[]{:S(2)}) collective-permute-start(bf16[2,512,256]{2,1,0:T(8,128)(2,1)S(1)} %pad_maximum_fusion.36), channel_id=1, source_target_pairs={{40,0},{48,8},{56,16},{64,24},{72,32},{80,40},{88,48},{96,56},{104... | collective-permute-start | bytes 1572872 | tf_op jit(solution)/shard_map/ppermute | solution.py:12
  602.6 97.5 %collective-permute-start.30 = (bf16[2,512,256]{2,1,0:T(8,128)(2,1)S(1)}, bf16[2,512,256]{2,1,0:T(8,128)(2,1)S(1)}, u32[]{:S(2)}, u32[]{:S(2)}) collective-permute-start(bf16[2,512,256]{2,1,0:T(8,128)(2,1)S(1)} %pad_maximum_fusion.36), channel_id=1, source_target_pairs={{0,88},{8,96},{16,104},{24,112},{32,120},{40,128},{48,136},{56,144... | collective-permute-start | bytes 1572872 | tf_op jit(solution)/shard_map/ppermute | solution.py:12
  635.3 68.9 %collective-permute-start.33 = (bf16[2,512,256]{2,1,0:T(8,128)(2,1)S(1)}, bf16[2,512,256]{2,1,0:T(8,128)(2,1)S(1)}, u32[]{:S(2)}, u32[]{:S(2)}) collective-permute-start(bf16[2,512,256]{2,1,0:T(8,128)(2,1)S(1)} %pad_maximum_fusion.37), channel_id=1, source_target_pairs={{168,0},{176,8},{184,16},{192,24},{200,32},{208,40},{216,48},{224,... | collective-permute-start | bytes 1572872 | tf_op jit(solution)/shard_map/ppermute | solution.py:12
  637.1 69.0 %collective-permute-start.3 = (bf16[2,512,256]{2,1,0:T(8,128)(2,1)S(1)}, bf16[2,512,256]{2,1,0:T(8,128)(2,1)S(1)}, u32[]{:S(2)}, u32[]{:S(2)}) collective-permute-start(bf16[2,512,256]{2,1,0:T(8,128)(2,1)S(1)} %pad_maximum_fusion.37), channel_id=1, source_target_pairs={{88,0},{96,8},{104,16},{112,24},{120,32},{128,40},{136,48},{144,56... | collective-permute-start | bytes 1572872 | tf_op jit(solution)/shard_map/ppermute | solution.py:12
  753.3 294.1 %all-reduce.6.cloned.1.call-start = ((), (), s32[]{:S(2)}) async-start(), calls=%async_computation.5 | async-start | bytes 524288 | tf_op jit(solution)/shard_map/psum | solution.py:179
  827.8 476.0 %all-reduce.4.cloned.1.call-start = ((), (), s32[]{:S(2)}) async-start(), calls=%async_computation.4 | async-start | bytes 524288 | tf_op jit(solution)/shard_map/psum | solution.py:180
  (110 other events, 4728.1 us)
Sparse Core Ops, SparseCore 0:
  11.2 53.4 all-gather.2
  72.7 82.5 reduce-scatter.1
  753.4 70.0 all-gather.4
  827.9 219.4 all-reduce.5
  1054.1 249.5 all-reduce.3
where the time goes:
time: 1330 us; the launch traced here: 1320 us
  waiting for transfers between devices  724 us (54%)
  starting transfers between devices  251 us (19%)
  blocking collectives  146 us (11%)
  other arithmetic  67.6 us (5%)
  matrix products  53.3 us (4%)
  local copies, waits for them, and re-layouts  42.2 us (3%)
  between operations  29.7 us (2%)
    psum x1, waiting for transfers between devices, local(): lax.psum((bilinear_part, loss_sum), ('tile', 'mlp'))  255 us
    ppermute x34, starting transfers between devices, shifted(): return lax.ppermute(array, axis, pairs)  251 us
    ppermute x34, waiting for transfers between devices, shifted(): return lax.ppermute(array, axis, pairs)  198 us
    psum x1, waiting for transfers between devices, local(): grad_in, grad_out = lax.psum((in_part, out_part), 'tile')  132 us
    psum x1, blocking collectives, local(): lax.psum((bilinear_part, loss_sum), ('tile', 'mlp'))  75.1 us
    reduce_scatter x1, waiting for transfers between devices, local(): lax.psum_scatter(jnp.einsum('rch,hf->rcf', active, w_out, preferred_eleme...  70.2 us
    all_gather x1, waiting for transfers between devices, local(): embed_whole = lax.all_gather(embed_grad, 'mlp', axis=0, tiled=True)  70.2 us
    all_gather x1, blocking collectives, local(): lax.all_gather(post_local, 'mlp', axis=0, tiled=True)  35.8 us
  transfers between devices with their start and end apart: 39, of which 16 were waited for; matrix products, arithmetic and copies ran while one was open for 9% of the time, Pallas kernels for 0%

commit v1 on v0

--- a/solution.py
+++ b/solution.py
@@ -4,6 +4,10 @@
 from jax.sharding import PartitionSpec as P
 
 column_plan = ((-1, 1), (0, 0), (0, 1), (1, 0))
+
+
+def lay_sector(vector):
+    return lax.psum(lax.psum(vector, "mlp"), "tile")
 
 
 def shifted(array, axis, by):
@@ -177,7 +181,7 @@
     in_part = jnp.einsum("rcf,rch->fh", whole_x, hidden_grad, preferred_element_type=jnp.float32)
     out_part = jnp.einsum("rch,rcf->hf", active, embed_whole, preferred_element_type=jnp.float32)
     grad_in, grad_out = lax.psum((in_part, out_part), "tile")
-    grad_bilinear, loss_total = lax.psum((bilinear_part, loss_sum), ("tile", "mlp"))
+    grad_bilinear, loss_total = lay_sector((bilinear_part, loss_sum))
     pair_loss = loss_total / (2.0 * tile_count * site_rows * 27 * site_rows)
     return (pair_loss, grad_in, grad_out, grad_bilinear)
 

time: 1330 us -> 1180 us (0.89)
  waiting for transfers between devices: 724 us -> 548 us
  starting transfers between devices: 251 us -> 275 us
    psum x1, waiting for transfers between devices: 255 us -> 86.1 us  [lay_sector(): return lax.psum(lax.psum(vector, 'mlp'), 'tile')]
    ppermute x34, starting transfers between devices: 251 us -> 275 us  [shifted(): return lax.ppermute(array, axis, pairs)]
    ppermute x34, waiting for transfers between devices: 198 us -> 182 us  [shifted(): return lax.ppermute(array, axis, pairs)]
    psum x1 -> x2, blocking collectives: 75.1 us -> 75.4 us  [lay_sector(): return lax.psum(lax.psum(vector, 'mlp'), 'tile')]
  transfers between devices with their start and end apart: 39 -> 39, of which waited for: 16 -> 15; matrix products, arithmetic and copies ran while one was open for 9% -> 10% of each run, Pallas kernels for 0% -> 0%
where the time goes in v1:
time: 1180 us; the launch traced here: 1160 us
  waiting for transfers between devices  548 us (46%)
  starting transfers between devices  275 us (23%)
  blocking collectives  147 us (12%)
  other arithmetic  67.9 us (6%)
  matrix products  56 us (5%)
  local copies, waits for them, and re-layouts  41.6 us (4%)
  between operations  29.5 us (2%)
    ppermute x34, starting transfers between devices, shifted(): return lax.ppermute(array, axis, pairs)  275 us
    ppermute x34, waiting for transfers between devices, shifted(): return lax.ppermute(array, axis, pairs)  182 us
    psum x1, waiting for transfers between devices, local(): grad_in, grad_out = lax.psum((in_part, out_part), 'tile')  137 us
    psum x1, waiting for transfers between devices, lay_sector(): return lax.psum(lax.psum(vector, 'mlp'), 'tile')  86.1 us
    psum x2, blocking collectives, lay_sector(): return lax.psum(lax.psum(vector, 'mlp'), 'tile')  75.4 us
    all_gather x1, waiting for transfers between devices, local(): embed_whole = lax.all_gather(embed_grad, 'mlp', axis=0, tiled=True)  72.4 us
    reduce_scatter x1, waiting for transfers between devices, local(): lax.psum_scatter(jnp.einsum('rch,hf->rcf', active, w_out, preferred_eleme...  70.1 us
    all_gather x1, blocking collectives, local(): lax.all_gather(post_local, 'mlp', axis=0, tiled=True)  35.9 us
  transfers between devices with their start and end apart: 39, of which 15 were waited for; matrix products, arithmetic and copies ran while one was open for 10% of the time, Pallas kernels for 0%

profile of v1, /device:TPU:2, one launch (start us, length us, event | category | flops | bytes accessed | tf_op | source)
XLA Modules:
  0.0 1164.8 jit_solution(15656909752436222987)
XLA Ops:
  85.4 70.1 %reduce-scatter.2.cloned.1.call-done = f32[64,4,256]{2,0,1:T(8,128)} async-done(((f32[512,4,256]{2,0,1:T(8,128)}), f32[64,4,256]{2,0,1:T(8,128)}) %reduce-scatter.2.cloned.1.call-update) | async-done | bytes 262160 | tf_op jit(solution)/shard_map/reduce_scatter | solution.py:57
  156.6 35.9 %all_gather.13 = bf16[512,2,256]{2,0,1:T(8,128)(2,1)S(1)} all-gather(bf16[64,2,256]{2,0,1:T(8,128)(2,1)S(1)} %slice.1000), channel_id=1, replica_groups=mesh['tile'=32,'mlp'=8] {'mlp'}, dimensions={0}, use_global_device_ids=true | all-gather | bytes 589824 | tf_op jit(solution)/shard_map/all_gather | solution.py:79
  192.7 35.5 %all_gather.14 = bf16[512,2,256]{2,0,1:T(8,128)(2,1)S(1)} all-gather(bf16[64,2,256]{2,0,1:T(8,128)(2,1)S(1)} %convolution_convert_fusion.1), channel_id=1, replica_groups=mesh['tile'=32,'mlp'=8] {'mlp'}, dimensions={0}, use_global_device_ids=true | all-gather | bytes 589824 | tf_op jit(solution)/shard_map/all_gather | solution.py:80
  246.6 10.0 collective-permute-done.5
  257.3 32.7 %collective-permute-done.6 = bf16[2,512,256]{2,1,0:T(8,128)(2,1)S(1)} collective-permute-done((bf16[2,512,256]{2,1,0:T(8,128)(2,1)S(1)}, bf16[2,512,256]{2,1,0:T(8,128)(2,1)S(1)}, u32[]{:S(2)}, u32[]{:S(2)}) %collective-permute-start.6) | collective-permute-done | bytes 524320 | tf_op jit(solution)/shard_map/ppermute | solution.py:16
  305.1 27.2 %collective-permute-done.2 = bf16[2,512,256]{2,1,0:T(8,128)(2,1)S(1)} collective-permute-done((bf16[2,512,256]{2,1,0:T(8,128)(2,1)S(1)}, bf16[2,512,256]{2,1,0:T(8,128)(2,1)S(1)}, u32[]{:S(2)}, u32[]{:S(2)}) %collective-permute-start.2) | collective-permute-done | bytes 524320 | tf_op jit(solution)/shard_map/ppermute | solution.py:16
  332.2 13.8 %collective-permute-start.13 = (bf16[2,512,256]{2,1,0:T(8,128)(2,1)S(1)}, bf16[2,512,256]{2,1,0:T(8,128)(2,1)S(1)}, u32[]{:S(2)}, u32[]{:S(2)}) collective-permute-start(bf16[2,512,256]{2,1,0:T(8,128)(2,1)S(1)} %pad_maximum_fusion.37), channel_id=1, source_target_pairs={{0,8},{8,16},{16,24},{24,32},{32,40},{40,48},{48,56},{56,64},{64,7... | collective-permute-start | bytes 1572872 | tf_op jit(solution)/shard_map/ppermute | solution.py:16
  349.5 13.4 %collective-permute-done.10 = bf16[2,512,256]{2,1,0:T(8,128)(2,1)S(1)} collective-permute-done((bf16[2,512,256]{2,1,0:T(8,128)(2,1)S(1)}, bf16[2,512,256]{2,1,0:T(8,128)(2,1)S(1)}, u32[]{:S(2)}, u32[]{:S(2)}) %collective-permute-start.10) | collective-permute-done | bytes 524320 | tf_op jit(solution)/shard_map/ppermute | solution.py:16
  365.0 37.0 %collective-permute-start.19 = (bf16[2,512,256]{2,1,0:T(8,128)(2,1)S(1)}, bf16[2,512,256]{2,1,0:T(8,128)(2,1)S(1)}, u32[]{:S(2)}, u32[]{:S(2)}) collective-permute-start(bf16[2,512,256]{2,1,0:T(8,128)(2,1)S(1)} %pad_maximum_fusion.37), channel_id=1, source_target_pairs={{8,0},{16,8},{24,16},{32,24},{40,32},{48,40},{56,48},{64,56},{72,6... | collective-permute-start | bytes 1572872 | tf_op jit(solution)/shard_map/ppermute | solution.py:16
  402.8 43.8 %collective-permute-start.20 = (bf16[2,512,256]{2,1,0:T(8,128)(2,1)S(1)}, bf16[2,512,256]{2,1,0:T(8,128)(2,1)S(1)}, u32[]{:S(2)}, u32[]{:S(2)}) collective-permute-start(bf16[2,512,256]{2,1,0:T(8,128)(2,1)S(1)} %pad_maximum_fusion.36), channel_id=1, source_target_pairs={{8,0},{16,8},{24,16},{32,24},{40,32},{48,40},{56,48},{64,56},{72,6... | collective-permute-start | bytes 1572872 | tf_op jit(solution)/shard_map/ppermute | solution.py:16
  487.9 24.7 %collective-permute-done.24 = bf16[2,512,256]{2,1,0:T(8,128)(2,1)S(1)} collective-permute-done((bf16[2,512,256]{2,1,0:T(8,128)(2,1)S(1)}, bf16[2,512,256]{2,1,0:T(8,128)(2,1)S(1)}, u32[]{:S(2)}, u32[]{:S(2)}) %collective-permute-start.24) | collective-permute-done | bytes 524320 | tf_op jit(solution)/shard_map/ppermute | solution.py:16
  512.6 24.1 %collective-permute-start.28 = (bf16[2,512,256]{2,1,0:T(8,128)(2,1)S(1)}, bf16[2,512,256]{2,1,0:T(8,128)(2,1)S(1)}, u32[]{:S(2)}, u32[]{:S(2)}) collective-permute-start(bf16[2,512,256]{2,1,0:T(8,128)(2,1)S(1)} %pad_maximum_fusion.36), channel_id=1, source_target_pairs={{32,0},{40,8},{48,16},{56,24},{64,32},{72,40},{80,48},{88,56},{96,... | collective-permute-start | bytes 1572872 | tf_op jit(solution)/shard_map/ppermute | solution.py:16
  538.8 12.6 %collective-permute-done.27 = bf16[2,512,256]{2,1,0:T(8,128)(2,1)S(1)} collective-permute-done((bf16[2,512,256]{2,1,0:T(8,128)(2,1)S(1)}, bf16[2,512,256]{2,1,0:T(8,128)(2,1)S(1)}, u32[]{:S(2)}, u32[]{:S(2)}) %collective-permute-start.27) | collective-permute-done | bytes 524320 | tf_op jit(solution)/shard_map/ppermute | solution.py:16
  556.2 12.1 %collective-permute-done.28 = bf16[2,512,256]{2,1,0:T(8,128)(2,1)S(1)} collective-permute-done((bf16[2,512,256]{2,1,0:T(8,128)(2,1)S(1)}, bf16[2,512,256]{2,1,0:T(8,128)(2,1)S(1)}, u32[]{:S(2)}, u32[]{:S(2)}) %collective-permute-start.28) | collective-permute-done | bytes 524320 | tf_op jit(solution)/shard_map/ppermute | solution.py:16
  573.2 13.2 %collective-permute-done.26 = bf16[2,512,256]{2,1,0:T(8,128)(2,1)S(1)} collective-permute-done((bf16[2,512,256]{2,1,0:T(8,128)(2,1)S(1)}, bf16[2,512,256]{2,1,0:T(8,128)(2,1)S(1)}, u32[]{:S(2)}, u32[]{:S(2)}) %collective-permute-start.26) | collective-permute-done | bytes 524320 | tf_op jit(solution)/shard_map/ppermute | solution.py:16
  589.4 54.6 %collective-permute-start.30 = (bf16[2,512,256]{2,1,0:T(8,128)(2,1)S(1)}, bf16[2,512,256]{2,1,0:T(8,128)(2,1)S(1)}, u32[]{:S(2)}, u32[]{:S(2)}) collective-permute-start(bf16[2,512,256]{2,1,0:T(8,128)(2,1)S(1)} %pad_maximum_fusion.36), channel_id=1, source_target_pairs={{0,88},{8,96},{16,104},{24,112},{32,120},{40,128},{48,136},{56,144... | collective-permute-start | bytes 1572872 | tf_op jit(solution)/shard_map/ppermute | solution.py:16
  653.1 27.9 %collective-permute-done.7 = bf16[2,512,256]{2,1,0:T(8,128)(2,1)S(1)} collective-permute-done((bf16[2,512,256]{2,1,0:T(8,128)(2,1)S(1)}, bf16[2,512,256]{2,1,0:T(8,128)(2,1)S(1)}, u32[]{:S(2)}, u32[]{:S(2)}) %collective-permute-start.7) | collective-permute-done | bytes 524320 | tf_op jit(solution)/shard_map/ppermute | solution.py:16
  681.0 13.2 %collective-permute-start.15 = (bf16[2,512,256]{2,1,0:T(8,128)(2,1)S(1)}, bf16[2,512,256]{2,1,0:T(8,128)(2,1)S(1)}, u32[]{:S(2)}, u32[]{:S(2)}) collective-permute-start(bf16[2,512,256]{2,1,0:T(8,128)(2,1)S(1)} %pad_maximum_fusion.37), channel_id=1, source_target_pairs={{120,0},{128,8},{136,16},{144,24},{152,32},{160,40},{168,48},{176,... | collective-permute-start | bytes 1572872 | tf_op jit(solution)/shard_map/ppermute | solution.py:16
  703.1 10.7 collective-permute-start.11
  764.1 72.4 %all-gather.5.cloned.1.call-done = bf16[512,4,256]{2,0,1:T(8,128)(2,1)} async-done(((bf16[64,4,256]{2,0,1:T(8,128)(2,1)}), bf16[512,4,256]{2,0,1:T(8,128)(2,1)}) %all-gather.5.cloned.1.call-update) | async-done | bytes 1048592 | tf_op jit(solution)/shard_map/all_gather | solution.py:177
  841.9 86.1 %all-reduce.4.cloned.1.call-done = f32[256,256]{1,0:T(8,128)} async-done(((f32[256,256]{1,0:T(8,128)}), f32[256,256]{1,0:T(8,128)}) %all-reduce.4.cloned.1.call-update) | async-done | bytes 262160 | tf_op jit(solution)/shard_map/psum | solution.py:10
  939.1 21.7 %psum.42 = f32[]{:T(128)} all-reduce(f32[]{:T(128)S(6)} %add.980), channel_id=1, replica_groups=mesh['tile'=32,'mlp'=8] {'mlp'}, use_global_device_ids=true, to_apply=%region_19.20 | all-reduce | flops 1 | bytes 8 | tf_op jit(solution)/shard_map/psum | solution.py:10
  960.8 53.6 %psum.43 = f32[]{:T(128)} all-reduce(f32[]{:T(128)} %psum.42), channel_id=1, replica_groups=mesh['tile'=32,'mlp'=8] {'tile'}, use_global_device_ids=true, to_apply=%region_20.21 | all-reduce | flops 1 | bytes 8 | tf_op jit(solution)/shard_map/psum | solution.py:10
  1015.1 136.8 %all-reduce.6.cloned.1.call-done = (f32[256,128]{0,1:T(8,128)}, f32[128,256]{1,0:T(8,128)}, f32[256,256]{1,0:T(8,128)}) async-done(((f32[256,128]{0,1:T(8,128)}, f32[128,256]{1,0:T(8,128)}, f32[256,256]{1,0:T(8,128)}), (f32[256,128]{0,1:T(8,128)}, f32[128,256]{1,0:T(8,128)}, f32[256,256]{1,0:T(8,128)})) %all-reduce.6.cloned.1.call-update) | async-done | bytes 524304 | tf_op jit(solution)/shard_map/psum | solution.py:183
  (469 shorter events, 252.1 us)
Async XLA Ops:
  7.2 62.2 %all-gather.3.cloned.1.call-start = ((), (), s32[]{:S(2)}) async-start(), calls=%async_computation.1 | async-start | bytes 1179648 | tf_op jit(solution)/shard_map/all_gather | solution.py:54
  8.9 146.7 %reduce-scatter.2.cloned.1.call-start = ((), (), s32[]{:S(2)}) async-start(), calls=%async_computation.2 | async-start | bytes 2359296 | tf_op jit(solution)/shard_map/reduce_scatter | solution.py:57
  72.9 763.6 %all-gather.5.cloned.1.call-start = ((), (), s32[]{:S(2)}) async-start(), calls=%async_computation.3 | async-start | bytes 1179648 | tf_op jit(solution)/shard_map/all_gather | solution.py:177
  241.6 62.7 %collective-permute-start.1 = (bf16[2,512,256]{2,1,0:T(8,128)(2,1)S(1)}, bf16[2,512,256]{2,1,0:T(8,128)(2,1)S(1)}, u32[]{:S(2)}, u32[]{:S(2)}) collective-permute-start(bf16[2,512,256]{2,1,0:T(8,128)(2,1)S(1)} %pad_maximum_fusion.37), channel_id=1, source_target_pairs={{0,40},{8,48},{16,56},{24,64},{32,72},{40,80},{48,88},{56,96},{64,... | collective-permute-start | bytes 1572872 | tf_op jit(solution)/shard_map/ppermute | solution.py:16
  243.5 88.7 %collective-permute-start.2 = (bf16[2,512,256]{2,1,0:T(8,128)(2,1)S(1)}, bf16[2,512,256]{2,1,0:T(8,128)(2,1)S(1)}, u32[]{:S(2)}, u32[]{:S(2)}) collective-permute-start(bf16[2,512,256]{2,1,0:T(8,128)(2,1)S(1)} %pad_maximum_fusion.36), channel_id=1, source_target_pairs={{0,40},{8,48},{16,56},{24,64},{32,72},{40,80},{48,88},{56,96},{64,... | collective-permute-start | bytes 1572872 | tf_op jit(solution)/shard_map/ppermute | solution.py:16
  256.6 89.5 %collective-permute-start = (bf16[2,512,256]{2,1,0:T(8,128)(2,1)S(1)}, bf16[2,512,256]{2,1,0:T(8,128)(2,1)S(1)}, u32[]{:S(2)}, u32[]{:S(2)}) collective-permute-start(bf16[2,512,256]{2,1,0:T(8,128)(2,1)S(1)} %pad_maximum_fusion.36), channel_id=1, source_target_pairs={{0,168},{8,176},{16,184},{24,192},{32,200},{40,208},{48,216},{56,2... | collective-permute-start | bytes 1572872 | tf_op jit(solution)/shard_map/ppermute | solution.py:16
  290.0 58.8 %collective-permute-start.9 = (bf16[2,512,256]{2,1,0:T(8,128)(2,1)S(1)}, bf16[2,512,256]{2,1,0:T(8,128)(2,1)S(1)}, u32[]{:S(2)}, u32[]{:S(2)}) collective-permute-start(bf16[2,512,256]{2,1,0:T(8,128)(2,1)S(1)} %pad_maximum_fusion.37), channel_id=1, source_target_pairs={{0,24},{8,32},{16,40},{24,48},{32,56},{40,64},{48,72},{56,80},{64,... | collective-permute-start | bytes 1572872 | tf_op jit(solution)/shard_map/ppermute | solution.py:16
  295.0 67.9 %collective-permute-start.10 = (bf16[2,512,256]{2,1,0:T(8,128)(2,1)S(1)}, bf16[2,512,256]{2,1,0:T(8,128)(2,1)S(1)}, u32[]{:S(2)}, u32[]{:S(2)}) collective-permute-start(bf16[2,512,256]{2,1,0:T(8,128)(2,1)S(1)} %pad_maximum_fusion.36), channel_id=1, source_target_pairs={{0,24},{8,32},{16,40},{24,48},{32,56},{40,64},{48,72},{56,80},{64,... | collective-permute-start | bytes 1572872 | tf_op jit(solution)/shard_map/ppermute | solution.py:16
  304.3 60.7 %collective-permute-start.8 = (bf16[2,512,256]{2,1,0:T(8,128)(2,1)S(1)}, bf16[2,512,256]{2,1,0:T(8,128)(2,1)S(1)}, u32[]{:S(2)}, u32[]{:S(2)}) collective-permute-start(bf16[2,512,256]{2,1,0:T(8,128)(2,1)S(1)} %pad_maximum_fusion.36), channel_id=1, source_target_pairs={{0,152},{8,160},{16,168},{24,176},{32,184},{40,192},{48,200},{56,2... | collective-permute-start | bytes 1572872 | tf_op jit(solution)/shard_map/ppermute | solution.py:16
  332.2 70.5 %collective-permute-start.13 = (bf16[2,512,256]{2,1,0:T(8,128)(2,1)S(1)}, bf16[2,512,256]{2,1,0:T(8,128)(2,1)S(1)}, u32[]{:S(2)}, u32[]{:S(2)}) collective-permute-start(bf16[2,512,256]{2,1,0:T(8,128)(2,1)S(1)} %pad_maximum_fusion.37), channel_id=1, source_target_pairs={{0,8},{8,16},{16,24},{24,32},{32,40},{40,48},{48,56},{56,64},{64,7... | collective-permute-start | bytes 1572872 | tf_op jit(solution)/shard_map/ppermute | solution.py:16
  346.1 101.2 %collective-permute-start.14 = (bf16[2,512,256]{2,1,0:T(8,128)(2,1)S(1)}, bf16[2,512,256]{2,1,0:T(8,128)(2,1)S(1)}, u32[]{:S(2)}, u32[]{:S(2)}) collective-permute-start(bf16[2,512,256]{2,1,0:T(8,128)(2,1)S(1)} %pad_maximum_fusion.36), channel_id=1, source_target_pairs={{0,8},{8,16},{16,24},{24,32},{32,40},{40,48},{48,56},{56,64},{64,7... | collective-permute-start | bytes 1572872 | tf_op jit(solution)/shard_map/ppermute | solution.py:16
  348.8 296.3 %collective-permute-start.12 = (bf16[2,512,256]{2,1,0:T(8,128)(2,1)S(1)}, bf16[2,512,256]{2,1,0:T(8,128)(2,1)S(1)}, u32[]{:S(2)}, u32[]{:S(2)}) collective-permute-start(bf16[2,512,256]{2,1,0:T(8,128)(2,1)S(1)} %pad_maximum_fusion.36), channel_id=1, source_target_pairs={{0,136},{8,144},{16,152},{24,160},{32,168},{40,176},{48,184},{56,1... | collective-permute-start | bytes 1572872 | tf_op jit(solution)/shard_map/ppermute | solution.py:16
  363.0 285.2 %collective-permute-start.16 = (bf16[2,512,256]{2,1,0:T(8,128)(2,1)S(1)}, bf16[2,512,256]{2,1,0:T(8,128)(2,1)S(1)}, u32[]{:S(2)}, u32[]{:S(2)}) collective-permute-start(bf16[2,512,256]{2,1,0:T(8,128)(2,1)S(1)} %pad_maximum_fusion.36), channel_id=1, source_target_pairs={{0,128},{8,136},{16,144},{24,152},{32,160},{40,168},{48,176},{56,1... | collective-permute-start | bytes 1572872 | tf_op jit(solution)/shard_map/ppermute | solution.py:16
  365.0 89.3 %collective-permute-start.19 = (bf16[2,512,256]{2,1,0:T(8,128)(2,1)S(1)}, bf16[2,512,256]{2,1,0:T(8,128)(2,1)S(1)}, u32[]{:S(2)}, u32[]{:S(2)}) collective-permute-start(bf16[2,512,256]{2,1,0:T(8,128)(2,1)S(1)} %pad_maximum_fusion.37), channel_id=1, source_target_pairs={{8,0},{16,8},{24,16},{32,24},{40,32},{48,40},{56,48},{64,56},{72,6... | collective-permute-start | bytes 1572872 | tf_op jit(solution)/shard_map/ppermute | solution.py:16
  402.8 56.2 %collective-permute-start.20 = (bf16[2,512,256]{2,1,0:T(8,128)(2,1)S(1)}, bf16[2,512,256]{2,1,0:T(8,128)(2,1)S(1)}, u32[]{:S(2)}, u32[]{:S(2)}) collective-permute-start(bf16[2,512,256]{2,1,0:T(8,128)(2,1)S(1)} %pad_maximum_fusion.36), channel_id=1, source_target_pairs={{8,0},{16,8},{24,16},{32,24},{40,32},{48,40},{56,48},{64,56},{72,6... | collective-permute-start | bytes 1572872 | tf_op jit(solution)/shard_map/ppermute | solution.py:16
  463.5 73.9 %collective-permute-start.22 = (bf16[2,512,256]{2,1,0:T(8,128)(2,1)S(1)}, bf16[2,512,256]{2,1,0:T(8,128)(2,1)S(1)}, u32[]{:S(2)}, u32[]{:S(2)}) collective-permute-start(bf16[2,512,256]{2,1,0:T(8,128)(2,1)S(1)} %pad_maximum_fusion.36), channel_id=1, source_target_pairs={{0,104},{8,112},{16,120},{24,128},{32,136},{40,144},{48,152},{56,1... | collective-permute-start | bytes 1572872 | tf_op jit(solution)/shard_map/ppermute | solution.py:16
  479.1 72.3 %collective-permute-start.27 = (bf16[2,512,256]{2,1,0:T(8,128)(2,1)S(1)}, bf16[2,512,256]{2,1,0:T(8,128)(2,1)S(1)}, u32[]{:S(2)}, u32[]{:S(2)}) collective-permute-start(bf16[2,512,256]{2,1,0:T(8,128)(2,1)S(1)} %pad_maximum_fusion.37), channel_id=1, source_target_pairs={{32,0},{40,8},{48,16},{56,24},{64,32},{72,40},{80,48},{88,56},{96,... | collective-permute-start | bytes 1572872 | tf_op jit(solution)/shard_map/ppermute | solution.py:16
  568.4 81.6 %collective-permute-start.31 = (bf16[2,512,256]{2,1,0:T(8,128)(2,1)S(1)}, bf16[2,512,256]{2,1,0:T(8,128)(2,1)S(1)}, u32[]{:S(2)}, u32[]{:S(2)}) collective-permute-start(bf16[2,512,256]{2,1,0:T(8,128)(2,1)S(1)} %pad_maximum_fusion.37), channel_id=1, source_target_pairs={{40,0},{48,8},{56,16},{64,24},{72,32},{80,40},{88,48},{96,56},{104... | collective-permute-start | bytes 1572872 | tf_op jit(solution)/shard_map/ppermute | solution.py:16
  586.4 112.5 %collective-permute-start.32 = (bf16[2,512,256]{2,1,0:T(8,128)(2,1)S(1)}, bf16[2,512,256]{2,1,0:T(8,128)(2,1)S(1)}, u32[]{:S(2)}, u32[]{:S(2)}) collective-permute-start(bf16[2,512,256]{2,1,0:T(8,128)(2,1)S(1)} %pad_maximum_fusion.36), channel_id=1, source_target_pairs={{40,0},{48,8},{56,16},{64,24},{72,32},{80,40},{88,48},{96,56},{104... | collective-permute-start | bytes 1572872 | tf_op jit(solution)/shard_map/ppermute | solution.py:16
  589.4 113.7 %collective-permute-start.30 = (bf16[2,512,256]{2,1,0:T(8,128)(2,1)S(1)}, bf16[2,512,256]{2,1,0:T(8,128)(2,1)S(1)}, u32[]{:S(2)}, u32[]{:S(2)}) collective-permute-start(bf16[2,512,256]{2,1,0:T(8,128)(2,1)S(1)} %pad_maximum_fusion.36), channel_id=1, source_target_pairs={{0,88},{8,96},{16,104},{24,112},{32,120},{40,128},{48,136},{56,144... | collective-permute-start | bytes 1572872 | tf_op jit(solution)/shard_map/ppermute | solution.py:16
  648.1 67.8 %collective-permute-start.33 = (bf16[2,512,256]{2,1,0:T(8,128)(2,1)S(1)}, bf16[2,512,256]{2,1,0:T(8,128)(2,1)S(1)}, u32[]{:S(2)}, u32[]{:S(2)}) collective-permute-start(bf16[2,512,256]{2,1,0:T(8,128)(2,1)S(1)} %pad_maximum_fusion.37), channel_id=1, source_target_pairs={{168,0},{176,8},{184,16},{192,24},{200,32},{208,40},{216,48},{224,... | collective-permute-start | bytes 1572872 | tf_op jit(solution)/shard_map/ppermute | solution.py:16
  650.0 67.9 %collective-permute-start.3 = (bf16[2,512,256]{2,1,0:T(8,128)(2,1)S(1)}, bf16[2,512,256]{2,1,0:T(8,128)(2,1)S(1)}, u32[]{:S(2)}, u32[]{:S(2)}) collective-permute-start(bf16[2,512,256]{2,1,0:T(8,128)(2,1)S(1)} %pad_maximum_fusion.37), channel_id=1, source_target_pairs={{88,0},{96,8},{104,16},{112,24},{120,32},{128,40},{136,48},{144,56... | collective-permute-start | bytes 1572872 | tf_op jit(solution)/shard_map/ppermute | solution.py:16
  763.1 164.9 %all-reduce.4.cloned.1.call-start = ((), (), s32[]{:S(2)}) async-start(), calls=%async_computation.4 | async-start | bytes 524288 | tf_op jit(solution)/shard_map/psum | solution.py:10
  764.1 387.8 %all-reduce.6.cloned.1.call-start = ((), (), s32[]{:S(2)}) async-start(), calls=%async_computation.5 | async-start | bytes 1048576 | tf_op jit(solution)/shard_map/psum | solution.py:183
  (109 other events, 4798.2 us)
Sparse Core Ops, SparseCore 0:
  11.2 53.4 all-gather.2
  73.0 82.5 reduce-scatter.1
  763.2 73.2 all-gather.4
  839.6 88.3 all-reduce.3
  931.4 220.4 all-reduce.5
